TPU v7x, 256 devices: a whole 4x4x8 slice. The times are simulated.
256 devices in a mesh: rep: 4 (over y_lo, core), dp: 64 (over z, x, y_hi).
Axes of the slice: x: 4, y: 4 (y_hi: 2, y_lo: 2; y = y_hi * 2 + y_lo), z: 8, core: 2. Of those that a mesh axis runs over, the one named last changes fastest.
Arguments:
- first_core: float32 [512, 512], P('dp'), may hold values from -6 to 6
- first_moment: float32 [512, 512], P('dp'), may hold values from -4 to 4
- first_second: float32 [512, 512], P('dp'), may hold values from 0.01 to 1
- mid_core: float32 [256, 131072], P('dp'), may hold values from -0.5 to 0.5
- mid_moment: float32 [256, 131072], P('dp'), may hold values from -4 to 4
- mid_second: float32 [256, 131072], P('dp'), may hold values from 0.01 to 1
- last_core: float32 [512, 512], P('dp'), may hold values from -0.5 to 0.5
- last_moment: float32 [512, 512], P('dp'), may hold values from -4 to 4
- last_second: float32 [512, 512], P('dp'), may hold values from 0.01 to 1
- cotangent: bfloat16 [4096, 128], P(('rep', 'dp')), may hold values from -6 to 6
- bag_lengths: int32 [256, 16], P(('rep', 'dp')), may hold values from 1 to 32, 256 in all within a row
- first_digit: int32 [65536], P(('rep', 'dp')), may hold values from 0 to 511
- mid_digit: int32 [65536, 1], P(('rep', 'dp')), may hold values from 0 to 255; in each aligned block of 256 rows (0 to 255, 256 to 511, ...) at most 2 rows name the same one
- last_digit: int32 [65536], P(('rep', 'dp')), may hold values from 0 to 511
Outputs:
- first_core_next: float32 [512, 512], P('dp')
- first_moment_next: float32 [512, 512], P('dp')
- first_second_next: float32 [512, 512], P('dp')
- mid_core_next: float32 [256, 131072], P('dp')
- mid_moment_next: float32 [256, 131072], P('dp')
- mid_second_next: float32 [256, 131072], P('dp')
- last_core_next: float32 [512, 512], P('dp')
- last_moment_next: float32 [512, 512], P('dp')
- last_second_next: float32 [512, 512], P('dp')
Inputs may be any that keep to these rules, and one draw needn't show every extreme that they name: `mid_digit`: within each block of 256 lookups no middle digit appears more than 2 times, and in some block one digit appears exactly 2 times. `bag_lengths`: each row sums to 256; some entry of each row equals 32.
All inputs are finite; a program needn't handle non-finite values.
Results may differ from a plain program's by a relative error of at most 0.0056.
Values may be sent and summed in bfloat16 or wider, within the bound.
No kernel may reach another device: no remote copies, remote signals or barrier semaphores. Data moves between devices by JAX's collectives and lax.ppermute only.
A program may use at most 64 MiB of HBM per device.

v0:
```python
import jax
import jax.numpy as jnp
from jax import lax
from jax.experimental import pallas as pl
from jax.experimental.pallas import tpu as pltpu
from jax.sharding import PartitionSpec as P


R = 128
D1 = 4
D2 = 8
D3 = 4
STEP = 20
CAP = 2
LANES = 128
N_SRC = 64
SLOTS = 512
GROUP = 32
GROUPS = 16

LEARN_RATE = 0.01
BETA_ONE = 0.9
BETA_TWO = 0.999
EPSILON = 1e-08

BF = jnp.bfloat16
F32 = jnp.float32
INTERPRET = False


def adam_update(current, moment, second, gradient):
    moment_next = BETA_ONE * moment + (1.0 - BETA_ONE) * gradient
    second_next = BETA_TWO * second + (1.0 - BETA_TWO) * gradient * gradient
    corrected = moment_next * (LEARN_RATE / (1.0 - BETA_ONE**STEP))
    spread = jnp.sqrt(second_next * (1.0 / (1.0 - BETA_TWO**STEP)))
    return (current - corrected / (spread + EPSILON), moment_next, second_next)


def iota(shape, axis):
    return lax.broadcasted_iota(jnp.int32, shape, axis)


def nn(a, b):
    return lax.dot_general(a, b, (((1,), (0,)), ((), ())), preferred_element_type=F32)


def nt(a, b):
    return lax.dot_general(a, b, (((1,), (1,)), ((), ())), preferred_element_type=F32)


def tn(a, b):
    return lax.dot_general(a, b, (((0,), (0,)), ((), ())), preferred_element_type=F32)


def ones_where(cond):
    return jnp.where(cond, 1.0, 0.0).astype(BF)


def split_two(x):
    hi = x.astype(BF)
    return hi, (x - hi.astype(F32)).astype(BF)


def pack_kernel(side_ref, mid_ref, first_ref, last_ref, bag_ref, cot_ref, fcore_ref, lcore_ref, out_ref):
    count = mid_ref.shape[1]
    mids = jnp.broadcast_to(mid_ref[...].astype(F32), (count, count))
    row, col = iota((count, count), 0), iota((count, count), 1)
    mid_column = jnp.sum(jnp.where(row == col, mids, 0.0), axis=1, keepdims=True)
    earlier = (mid_column == mids) & (row < col)
    rank = jnp.sum(jnp.where(earlier, 1.0, 0.0), axis=0, keepdims=True)
    slot = mid_ref[...] * CAP + rank.astype(jnp.int32)
    place = ones_where(iota((SLOTS, count), 0) == slot)

    samples = bag_ref.shape[1]
    lens = jnp.broadcast_to(bag_ref[...].astype(F32), (samples, samples))
    n_row, n_col = iota((samples, samples), 0), iota((samples, samples), 1)
    ends = jnp.sum(jnp.where(n_col <= n_row, lens, 0.0), axis=1, keepdims=True)
    starts = jnp.sum(jnp.where(n_col < n_row, lens, 0.0), axis=1, keepdims=True)
    position = iota((samples, count), 1).astype(F32)
    owner = ones_where((position >= starts) & (position < ends))
    slot_owner = nt(place, owner).astype(BF)
    out_ref[:, 0:LANES] = nn(slot_owner, cot_ref[...]).astype(BF)

    field = iota((LANES, count), 0)
    first, last = first_ref[...], last_ref[...]
    fields = jnp.where(field == 0, first // 32, 0)
    fields = jnp.where(field == 1, first % 32, fields)
    fields = jnp.where(field == 2, last // 32, fields)
    fields = jnp.where(field == 3, last % 32, fields)
    out_ref[:, LANES : 2 * LANES] = nt(place, fields.astype(F32).astype(BF)).astype(BF)

    side = side_ref[0]
    width = fcore_ref.shape[1]
    core = jnp.where(side == 0, fcore_ref[...], lcore_ref[...])
    core = jnp.concatenate([core, core], axis=0).astype(BF)
    dest = iota((width, width), 1)
    source = jnp.where(side == 0, dest, (dest % LANES) * D3 + dest // LANES)
    core = nn(core, ones_where(iota((width, width), 0) == source)).astype(BF)
    for p in range(SLOTS // 16):
        out_ref[p * 16 : p * 16 + 16, 2 * LANES : 2 * LANES + width] = core


def pack(side, mid_digit, first_digit, last_digit, bag, cot, first_core, last_core):
    vmem = pl.BlockSpec(memory_space=pltpu.VMEM)
    return pl.pallas_call(
        pack_kernel,
        out_shape=jax.ShapeDtypeStruct((SLOTS, 2 * LANES + first_core.shape[1]), BF),
        in_specs=[pl.BlockSpec(memory_space=pltpu.SMEM)] + [vmem] * 7,
        out_specs=vmem,
        interpret=INTERPRET,
        name="pack",
    )(side, mid_digit, first_digit, last_digit, bag, cot, first_core, last_core)


def terms_kernel(
    side_ref, mine_ref, theirs_ref, mid_ref,
    midkeep_ref, midsend_ref, keep_ref, send_ref,
    cores, lrows, pick, diag, mix_hi, mix_lo, outer, chosen, asub,
):
    side = side_ref[0]
    cores[side] = mine_ref[:, 2 * LANES :]
    cores[1 - side] = theirs_ref[:, 2 * LANES :]
    up, across = iota((SLOTS, SLOTS), 0), iota((SLOTS, SLOTS), 1)
    source = (up // GROUP % 2) * GROUP + up % GROUP
    slots = nn(ones_where(across == source * 8 + up // (2 * GROUP)), mine_ref[:, 0 : 2 * LANES])
    grads = slots[:, 0:LANES].astype(BF)
    first = slots[:, LANES : LANES + 1] * 32.0 + slots[:, LANES + 1 : LANES + 2]
    last = slots[:, LANES + 2 : LANES + 3] * 32.0 + slots[:, LANES + 3 : LANES + 4]
    across_f = across.astype(F32)
    pick_first = ones_where(across_f == first)
    pick_last = ones_where(across_f == last)
    chosen[side] = pick_first
    chosen[1 - side] = pick_last
    arows = nn(pick_first, cores[0]).astype(BF)
    last_rows = nn(pick_last, cores[1]).astype(BF)
    for q in range(GROUPS):
        for c in range(D3):
            lrows[q, c * GROUP : (c + 1) * GROUP, :] = last_rows[
                q * GROUP : (q + 1) * GROUP, c * LANES : (c + 1) * LANES
            ]
        for a in range(D1):
            asub[q, a * GROUP : (a + 1) * GROUP, :] = arows[
                q * GROUP : (q + 1) * GROUP, a * R : (a + 1) * R
            ]

    pick[...] = jnp.zeros(pick.shape, BF)
    tile_row, tile_lane = iota((16, LANES), 0), iota((16, LANES), 1)
    for ab in range(D1 * D2):
        pick[ab, (ab // 4) * 16 : (ab // 4) * 16 + 16, :] = ones_where(
            tile_row == D3 * (ab % 4) + tile_lane // GROUP
        )
    own = ones_where(iota((SLOTS, 2 * LANES), 0) % GROUP == iota((SLOTS, 2 * LANES), 1) % GROUP)

    def spread(step, carry):
        for part in range(4):
            ab = step * 8 + part * 2
            pair = jnp.concatenate([pick[ab], pick[ab + 1]], axis=1)
            value = nn(grads, pair).astype(BF) * own
            diag[ab] = value[:, 0:LANES]
            diag[ab + 1] = value[:, LANES:]
        return carry

    lax.fori_loop(0, D1 * D2 // 8, spread, 0)

    def row(m, carry):
        left = jnp.concatenate([asub[4 * m + g] for g in range(4)], axis=0)
        totals = [None] * 4
        for b in range(0, D2, 2):
            heads = [
                lax.dot_general(
                    mid_ref[m, b + i], left, (((0,), (1,)), ((), ())), preferred_element_type=F32
                ).astype(BF)
                for i in range(2)
            ]
            for g in range(4):
                q = 4 * m + g
                here = pl.ds(pl.multiple_of(q * GROUP, GROUP), GROUP)
                there = pl.ds(pl.multiple_of(q * D1 * GROUP, D1 * GROUP), D1 * GROUP)
                block = jnp.concatenate(
                    [diag[a * D2 + b + i, here, :] for i in range(2) for a in range(D1)], axis=0
                )
                head = jnp.concatenate([h[:, g * LANES : (g + 1) * LANES] for h in heads], axis=1)
                part = nn(head, block)
                totals[g] = part if totals[g] is None else totals[g] + part
                hi, lo = split_two(nn(block, lrows[q]))
                for i in range(2):
                    mix_hi[b + i, there, :] = hi[i * LANES : (i + 1) * LANES]
                    mix_lo[b + i, there, :] = lo[i * LANES : (i + 1) * LANES]
        for g in range(4):
            here = pl.ds(pl.multiple_of((4 * m + g) * GROUP, GROUP), GROUP)
            total = totals[g].T
            for c in range(D3):
                outer[1 - side, c, here, :] = total[c * GROUP : (c + 1) * GROUP, :]
        return carry

    lax.fori_loop(0, 4, row, 0)

    for n in range(4):
        half = side if n < 2 else 1 - side
        m = half * 2 + n % 2
        grad_ref = midkeep_ref if n < 2 else midsend_ref
        span = pl.ds(pl.multiple_of(m * SLOTS, SLOTS), SLOTS)
        left = jnp.concatenate([asub[4 * m + g] for g in range(4)], axis=0)
        part = None
        for b in range(0, D2, 2):
            hi = jnp.concatenate([mix_hi[b, span, :], mix_hi[b + 1, span, :]], axis=1)
            lo = jnp.concatenate([mix_lo[b, span, :], mix_lo[b + 1, span, :]], axis=1)
            pair = jnp.concatenate([mid_ref[m, b], mid_ref[m, b + 1]], axis=1)
            term = nt(jnp.concatenate([hi, lo], axis=1), jnp.concatenate([pair, pair], axis=1))
            part = term if part is None else part + term
            grad = tn(left, hi)
            for h in range(2):
                tops = slice(h * (R // 2), (h + 1) * (R // 2))
                grad_ref[h, n % 2, b] = grad[tops, 0:LANES]
                grad_ref[h, n % 2, b + 1] = grad[tops, LANES:]
        for q in range(4):
            for a in range(D1):
                here = pl.ds(pl.multiple_of((4 * m + q) * GROUP, GROUP), GROUP)
                outer[side, a, here, :] = part[(q * D1 + a) * GROUP : (q * D1 + a + 1) * GROUP, :]

    for n, ref in ((1, send_ref), (0, keep_ref)):
        for a in range(0, D1, 2):
            hi, lo = split_two(jnp.concatenate([outer[n, a], outer[n, a + 1]], axis=1))
            ref[:, a * LANES : (a + 2) * LANES] = tn(chosen[n], hi) + tn(chosen[n], lo)


def terms(side, mine, theirs, mid):
    vmem = pl.BlockSpec(memory_space=pltpu.VMEM)
    width = D1 * R
    half = (2, 2, D2, R // 2, LANES)
    return pl.pallas_call(
        terms_kernel,
        out_shape=(
            jax.ShapeDtypeStruct(half, F32),
            jax.ShapeDtypeStruct(half, F32),
            jax.ShapeDtypeStruct((SLOTS, width), F32),
            jax.ShapeDtypeStruct((SLOTS, width), F32),
        ),
        in_specs=[pl.BlockSpec(memory_space=pltpu.SMEM)] + [vmem] * 3,
        out_specs=(vmem,) * 4,
        scratch_shapes=[
            pltpu.VMEM((2, SLOTS, width), BF),
            pltpu.VMEM((GROUPS, D3 * GROUP, LANES), BF),
            pltpu.VMEM((D1 * D2, LANES, LANES), BF),
            pltpu.VMEM((D1 * D2, SLOTS, LANES), BF),
            pltpu.VMEM((D2, 4 * SLOTS, LANES), BF),
            pltpu.VMEM((D2, 4 * SLOTS, LANES), BF),
            pltpu.VMEM((2, D1, SLOTS, LANES), F32),
            pltpu.VMEM((2, SLOTS, SLOTS), BF),
            pltpu.VMEM((GROUPS, D1 * GROUP, R), BF),
        ],
        interpret=INTERPRET,
        name="terms",
    )(side, mine, theirs, mid)


R_BLOCK = 16


def mid_copy_kernel(core_ref, out_ref):
    for m in range(4):
        for b in range(D2):
            out_ref[m, b] = core_ref[pl.ds(b * 4 + m, R_BLOCK, stride=4 * D2), :].astype(BF)


def mid_round(core):
    return pl.pallas_call(
        mid_copy_kernel,
        grid=(R // R_BLOCK,),
        out_shape=jax.ShapeDtypeStruct((4, D2, R, LANES), BF),
        in_specs=[pl.BlockSpec((R_BLOCK * D2 * 4, LANES), lambda i: (i, 0))],
        out_specs=pl.BlockSpec((4, D2, R_BLOCK, LANES), lambda i: (0, 0, i, 0)),
        interpret=INTERPRET,
        name="mid_round",
    )(core)


def mid_kernel(
    side_ref, core_ref, moment_ref, second_ref, near_ref, far_ref, near_rest_ref, far_rest_ref, *refs
):
    core_out, moment_out, second_out, grad = refs[-4:]
    side = side_ref[0]
    for i in range(2):
        for b in range(D2):
            own = near_ref[i, b].astype(F32) + far_ref[i, b].astype(F32)
            rest = near_rest_ref[i, b].astype(F32) + far_rest_ref[i, b].astype(F32)
            at = b * 4 + i
            grad[pl.ds(at + side * 2, R_BLOCK, stride=4 * D2), :] = own
            grad[pl.ds(at + (1 - side) * 2, R_BLOCK, stride=4 * D2), :] = rest
    core, moment, second = adam_update(core_ref[...], moment_ref[...], second_ref[...], grad[...])
    core_out[...] = core
    moment_out[...] = moment
    second_out[...] = second


def mid_step(side, states, parts, h, begun):
    rows = R_BLOCK * D2 * 4
    blocks = R // R_BLOCK // 2
    state = pl.BlockSpec((rows, LANES), lambda i: (i + h * blocks, 0))
    part = pl.BlockSpec((2, D2, R_BLOCK, LANES), lambda i: (0, 0, i, 0))
    untouched = [pl.BlockSpec(memory_space=pl.ANY)] * len(begun)
    return pl.pallas_call(
        mid_kernel,
        grid=(blocks,),
        out_shape=tuple(jax.ShapeDtypeStruct(states[0].shape, F32) for _ in range(3)),
        in_specs=[pl.BlockSpec(memory_space=pltpu.SMEM)] + [state] * 3 + [part] * 4 + untouched,
        out_specs=(state,) * 3,
        input_output_aliases={8 + n: n for n in range(len(begun))},
        scratch_shapes=[pltpu.VMEM((rows, LANES), F32)],
        interpret=INTERPRET,
        name="mid_step",
    )(side, *states, *parts, *begun)


def outer_kernel(side_ref, own_ref, chip_ref, core_ref, both_ref, *refs):
    side = side_ref[0]
    mine = own_ref[...] + chip_ref[...]
    theirs = core_ref[...] + both_ref[...]
    first_grad = jnp.where(side == 0, mine, theirs)
    last_grad = jnp.where(side == 0, theirs, mine)
    width = mine.shape[1]
    dest = iota((width, width), 1)
    source = (dest % D3) * LANES + dest // D3
    order = ones_where(iota((width, width), 0) == source)
    hi = last_grad.astype(BF)
    rest = last_grad - hi.astype(F32)
    low, lowest = split_two(rest)
    moved = nn(jnp.concatenate([hi, low, lowest], axis=0), order)
    count = mine.shape[0]
    last_grad = moved[:count] + (moved[count : 2 * count] + moved[2 * count :])
    f_next = adam_update(refs[0][...], refs[1][...], refs[2][...], first_grad)
    l_next = adam_update(refs[3][...], refs[4][...], refs[5][...], last_grad)
    for ref, value in zip(refs[6:], f_next + l_next):
        ref[...] = value


def outer_step(side, shares, states):
    vmem = pl.BlockSpec(memory_space=pltpu.VMEM)
    mine = shares[0]
    return pl.pallas_call(
        outer_kernel,
        out_shape=tuple(jax.ShapeDtypeStruct(mine.shape, F32) for _ in range(6)),
        in_specs=[pl.BlockSpec(memory_space=pltpu.SMEM)] + [vmem] * 10,
        out_specs=(vmem,) * 6,
        interpret=INTERPRET,
        name="outer",
    )(side, *shares, *states)


def row_tiles(x):
    return x.reshape(4, D2 * R, LANES).transpose(1, 0, 2).reshape(4 * D2 * R, LANES)


def untile(x):
    return x.reshape(D2 * R, 4, LANES).transpose(1, 0, 2).reshape(4, D2 * R * LANES)


CORE_SWAP = ((0, 1), (1, 0), (2, 3), (3, 2))
CHIP_SWAP = ((0, 2), (2, 0), (1, 3), (3, 1))
BOTH_SWAP = ((0, 3), (3, 0), (1, 2), (2, 1))


def local(
    first_core,
    first_moment,
    first_second,
    mid_core,
    mid_moment,
    mid_second,
    last_core,
    last_moment,
    last_second,
    cotangent,
    bag_lengths,
    first_digit,
    mid_digit,
    last_digit,
):
    side = (lax.axis_index("rep") % 2).astype(jnp.int32).reshape(1)
    packed = pack(
        side,
        mid_digit.reshape(1, -1),
        first_digit.reshape(1, -1),
        last_digit.reshape(1, -1),
        bag_lengths,
        cotangent,
        first_core,
        last_core,
    )
    mid_rows = row_tiles(mid_core)
    mine = lax.all_to_all(packed, "dp", split_axis=0, concat_axis=0, tiled=True)
    mid_copy = mid_round(mid_rows)
    theirs = lax.ppermute(mine, "rep", CORE_SWAP)
    mid_keep, mid_send, keep, send = terms(side, mine, theirs, mid_copy)

    mid_other = lax.ppermute(mid_send, "rep", CORE_SWAP)
    other = lax.ppermute(send, "rep", CORE_SWAP)
    near = [(mid_keep[h] + mid_other[h]).astype(BF) for h in range(2)]
    *near, chip_sum = lax.optimization_barrier((*near, (keep + other).astype(BF)))
    states = (mid_rows, row_tiles(mid_moment), row_tiles(mid_second))
    mid_next = ()
    far = []
    for h in range(2):
        far.append(lax.ppermute(near[h], "rep", CHIP_SWAP))
    share = lax.all_to_all(chip_sum, "dp", split_axis=0, concat_axis=0, tiled=True)
    for h in range(2):
        near_rest = lax.ppermute(near[h], "rep", CORE_SWAP)
        far_rest = lax.ppermute(far[h], "rep", CORE_SWAP)
        mid_next = mid_step(side, states, (near[h], far[h], near_rest, far_rest), h, mid_next)

    share, *mid_next = lax.optimization_barrier((share, *mid_next))
    mid_next = tuple(untile(x) for x in mid_next)
    share = jnp.sum(share.reshape(N_SRC, -1, share.shape[1]).astype(F32), axis=0)
    swapped = tuple(
        lax.ppermute(share, "rep", pairs) for pairs in (CHIP_SWAP, CORE_SWAP, BOTH_SWAP)
    )
    outer = outer_step(
        side,
        (share,) + swapped,
        (first_core, first_moment, first_second, last_core, last_moment, last_second),
    )
    return outer[:3] + mid_next + outer[3:]


def solution(mesh):
    rows = P("dp", None)
    spread = P(("rep", "dp"), None)
    flat = P(("rep", "dp"))
    return jax.shard_map(
        local,
        mesh=mesh,
        in_specs=(rows,) * 9 + (spread, spread, flat, spread, flat),
        out_specs=(rows,) * 9,
        check_vma=False,
    )
```

profile of v0, /device:TPU:1, one launch (start us, length us, event | category | flops | bytes accessed | tf_op | source)
XLA Modules:
  0.0 114.5 jit_solution(14092998827597808566)
XLA Ops:
  0.7 2.4 %pack.1 = bf16[512,768]{1,0:T(8,128)(2,1)} custom-call(s32[1]{0:T(128)} %bitcast.side_ref, s32[1,256]{1,0:T(1,128)} %bitcast.59, s32[1,256]{1,0:T(1,128)} %bitcast.60, s32[1,256]{1,0:T(1,128)} %bitcast.61, s32[1,16]{1,0:T(1,128)} %bag_ref.1, bf16[16,128]{1,0:T(8,128)(2,1)} %cot_ref.1, f32[8,512]{1,0:T(8,128)} %refs_0_.1, f32[8,512]{1,0:T(8,128)} %refs_3_.1), custom_call_target="tpu_custom_call" | custom-call | tf_op jit(solution)/shard_map/pack/pallas_call | solution.py:105
  3.0 37.6 %all_to_all.23 = bf16[64,8,768]{2,1,0:T(8,128)(2,1)S(1)} all-to-all(bf16[64,8,768]{2,1,0:T(8,128)(2,1)} %bitcast.52), channel_id=1, replica_groups=mesh['rep'=4,'dp'=64] {'dp'}, dimensions={0} | all-to-all | bytes 1572864 | tf_op jit(solution)/shard_map/all_to_all | solution.py:391
  40.7 2.9 %collective-permute-start = (bf16[512,768]{1,0:T(8,128)(2,1)S(1)}, bf16[512,768]{1,0:T(8,128)(2,1)S(1)}, u32[]{:S(2)}, u32[]{:S(2)}) collective-permute-start(bf16[512,768]{1,0:T(8,128)(2,1)S(1)} %bitcast.53), channel_id=1, source_target_pairs={{0,64},{64,0},{128,192},{192,128},{1,65},{65,1},{129,193},{193,129... | collective-permute-start | bytes 2359304 | tf_op jit(solution)/shard_map/ppermute | solution.py:393
  43.5 5.9 %mid_round.1.mid_ref = bf16[4,8,128,128]{3,2,1,0:T(8,128)(2,1)} custom-call(f32[4096,128]{1,0:T(8,128)} %bitcast.45), custom_call_target="tpu_custom_call" | custom-call | tf_op jit(solution)/shard_map/mid_round/pallas_call | solution.py:267
  49.4 0.9 copy-done.4
  50.3 15.3 %terms.1 = (f32[2,2,8,64,128]{4,3,2,1,0:T(8,128)}, f32[2,2,8,64,128]{4,3,2,1,0:T(8,128)}, f32[512,512]{1,0:T(8,128)}, f32[512,512]{1,0:T(8,128)}) custom-call(s32[1]{0:T(128)} %bitcast.side_ref, bf16[512,768]{1,0:T(8,128)(2,1)} %bitcast.54, bf16[512,768]{1,0:T(8,128)(2,1)} %copy-done.4, bf16[4,8,128,128]{3,2,1,0:T(8,128)(2,1)} %mid_round.1.mid_ref), custom_call_target="tpu_custom_call" | custom-call | tf_op jit(solution)/shard_map/terms/pallas_call | solution.py:231
  66.2 2.4 %collective-permute-done.1 = f32[2,2,8,64,128]{4,3,2,1,0:T(8,128)S(1)} collective-permute-done((f32[2,2,8,64,128]{4,3,2,1,0:T(8,128)}, f32[2,2,8,64,128]{4,3,2,1,0:T(8,128)S(1)}, u32[]{:S(2)}, u32[]{:S(2)}) %collective-permute-start.1) | collective-permute-done | bytes 1048608 | tf_op jit(solution)/shard_map/ppermute | solution.py:396
  68.6 1.4 %fusion.3 = (bf16[2,8,64,128]{3,2,1,0:T(8,128)(2,1)S(1)}, bf16[2,8,64,128]{3,2,1,0:T(8,128)(2,1)S(1)}) fusion(f32[2,2,8,64,128]{4,3,2,1,0:T(8,128)S(1)} %collective-permute-done.1, f32[2,2,8,64,128]{4,3,2,1,0:T(8,128)} %get-tuple-element.32), kind=kLoop, calls=%fused_computation.7 | loop fusion | flops 524288 | bytes 2621440 | tf_op jit(solution)/shard_map/convert_element_type | solution.py:398
  70.1 1.0 add_convert_fusion
  71.0 5.9 %all-to-all-start.1 = ((bf16[64,8,512]{2,1,0:T(8,128)(2,1)}), bf16[64,8,512]{2,1,0:T(8,128)(2,1)S(1)}, u32[]{:S(2)}, u32[]{:S(2)}) async-start(bf16[64,8,512]{2,1,0:T(8,128)(2,1)} %bitcast.11), calls=%async_computation.1 | async-start | bytes 1048576 | tf_op jit(solution)/shard_map/all_to_all | solution.py:405
  77.4 1.1 collective-permute-start.3
  78.5 1.0 collective-permute-start.7
  79.5 8.0 %collective-permute-done.6.far_ref = bf16[2,8,64,128]{3,2,1,0:T(8,128)(2,1)S(1)} collective-permute-done((bf16[2,8,64,128]{3,2,1,0:T(8,128)(2,1)S(1)}, bf16[2,8,64,128]{3,2,1,0:T(8,128)(2,1)S(1)}, u32[]{:S(2)}, u32[]{:S(2)}) %collective-permute-start.6) | collective-permute-done | bytes 262176 | tf_op jit(solution)/shard_map/ppermute | solution.py:404
  87.5 2.8 %collective-permute-start.8 = (bf16[2,8,64,128]{3,2,1,0:T(8,128)(2,1)S(1)}, bf16[2,8,64,128]{3,2,1,0:T(8,128)(2,1)S(1)}, u32[]{:S(2)}, u32[]{:S(2)}) collective-permute-start(bf16[2,8,64,128]{3,2,1,0:T(8,128)(2,1)S(1)} %collective-permute-done.6.far_ref), channel_id=1, source_target_pairs={{0,64},{64,0},{128,192},{192,128},{1,65},{65,1},{129,193},{193,129... | collective-permute-start | bytes 786440 | tf_op jit(solution)/shard_map/ppermute | solution.py:408
  90.4 5.2 %collective-permute-done.3.far_ref = bf16[2,8,64,128]{3,2,1,0:T(8,128)(2,1)S(1)} collective-permute-done((bf16[2,8,64,128]{3,2,1,0:T(8,128)(2,1)S(1)}, bf16[2,8,64,128]{3,2,1,0:T(8,128)(2,1)S(1)}, u32[]{:S(2)}, u32[]{:S(2)}) %collective-permute-start.3) | collective-permute-done | bytes 262176 | tf_op jit(solution)/shard_map/ppermute | solution.py:404
  95.5 1.2 %collective-permute-start.5 = (bf16[2,8,64,128]{3,2,1,0:T(8,128)(2,1)S(1)}, bf16[2,8,64,128]{3,2,1,0:T(8,128)(2,1)S(1)}, u32[]{:S(2)}, u32[]{:S(2)}) collective-permute-start(bf16[2,8,64,128]{3,2,1,0:T(8,128)(2,1)S(1)} %collective-permute-done.3.far_ref), channel_id=1, source_target_pairs={{0,64},{64,0},{128,192},{192,128},{1,65},{65,1},{129,193},{193,129... | collective-permute-start | bytes 786440 | tf_op jit(solution)/shard_map/ppermute | solution.py:408
  96.7 0.7 copy-done.9
  97.5 4.9 %mid_step.2 = (f32[4096,128]{1,0:T(8,128)}, f32[4096,128]{1,0:T(8,128)}, f32[4096,128]{1,0:T(8,128)}) custom-call(s32[1]{0:T(128)} %bitcast.side_ref, f32[4096,128]{1,0:T(8,128)} %bitcast.46, f32[4096,128]{1,0:T(8,128)} %bitcast.48, f32[4096,128]{1,0:T(8,128)} %bitcast.50, bf16[2,8,64,128]{3,2,1,0:T(8,128)(2,1)} %copy-done.3, ...), custom_call_target="tpu_custom_call" | custom-call | tf_op jit(solution)/shard_map/mid_step/pallas_call | solution.py:302
  102.5 0.7 copy-done.6
  103.3 4.9 %mid_step.3 = (f32[4096,128]{1,0:T(8,128)}, f32[4096,128]{1,0:T(8,128)}, f32[4096,128]{1,0:T(8,128)}) custom-call(s32[1]{0:T(128)} %bitcast.side_ref, f32[4096,128]{1,0:T(8,128)} %bitcast.47, f32[4096,128]{1,0:T(8,128)} %bitcast.49, f32[4096,128]{1,0:T(8,128)} %bitcast.51, ...), custom_call_target="tpu_custom_call", output_to_operand_aliasing={{0}: (8, {}), {1}: (9, {}), {2}: (10, {})} | custom-call | tf_op jit(solution)/shard_map/mid_step/pallas_call | solution.py:302
  109.4 0.9 collective-permute-start.9
  110.3 1.3 %collective-permute-done.11.both_ref = f32[8,512]{1,0:T(8,128)S(1)} collective-permute-done((f32[8,512]{1,0:T(8,128)S(1)}, f32[8,512]{1,0:T(8,128)S(1)}, u32[]{:S(2)}, u32[]{:S(2)}) %collective-permute-start.11) | collective-permute-done | bytes 16416 | tf_op jit(solution)/shard_map/ppermute | solution.py:415
  112.2 0.6 copy-done.14
  112.8 1.7 %outer.1 = (f32[8,512]{1,0:T(8,128)}, f32[8,512]{1,0:T(8,128)}, f32[8,512]{1,0:T(8,128)}, f32[8,512]{1,0:T(8,128)}, f32[8,512]{1,0:T(8,128)}, /*index=5*/f32[8,512]{1,0:T(8,128)}) custom-call(s32[1]{0:T(128)} %bitcast.side_ref, f32[8,512]{1,0:T(8,128)} %copy-done.11, f32[8,512]{1,0:T(8,128)} %copy-done.14, f32[8,512]{1,0:T(8,128)} %copy-done.13, ...), custom_call_target="tpu_custom_call" | custom-call | tf_op jit(solution)/shard_map/outer/pallas_call | solution.py:340
  (42 shorter events, 3.2 us)
Async XLA Ops:
  40.7 8.8 %copy-start = (bf16[64,8,768]{2,1,0:T(8,128)(2,1)}, bf16[64,8,768]{2,1,0:T(8,128)(2,1)S(1)}, u32[]{:S(2)}) copy-start(bf16[64,8,768]{2,1,0:T(8,128)(2,1)S(1)} %all_to_all.23) | copy-start | bytes 2359300
  40.7 8.8 %collective-permute-start = (bf16[512,768]{1,0:T(8,128)(2,1)S(1)}, bf16[512,768]{1,0:T(8,128)(2,1)S(1)}, u32[]{:S(2)}, u32[]{:S(2)}) collective-permute-start(bf16[512,768]{1,0:T(8,128)(2,1)S(1)} %bitcast.53), channel_id=1, source_target_pairs={{0,64},{64,0},{128,192},{192,128},{1,65},{65,1},{129,193},{193,129... | collective-permute-start | bytes 2359304 | tf_op jit(solution)/shard_map/ppermute | solution.py:393
  49.4 0.9 copy-start.4
  65.7 4.4 %copy-start.2 = (f32[512,512]{1,0:T(8,128)S(1)}, f32[512,512]{1,0:T(8,128)}, u32[]{:S(2)}) copy-start(f32[512,512]{1,0:T(8,128)} %get-tuple-element.34) | copy-start | bytes 3145732
  65.7 2.9 %collective-permute-start.1 = (f32[2,2,8,64,128]{4,3,2,1,0:T(8,128)}, f32[2,2,8,64,128]{4,3,2,1,0:T(8,128)S(1)}, u32[]{:S(2)}, u32[]{:S(2)}) collective-permute-start(f32[2,2,8,64,128]{4,3,2,1,0:T(8,128)} %get-tuple-element.33), channel_id=1, source_target_pairs={{0,64},{64,0},{128,192},{192,128},{1,65},{65,1},{129,193},{193,129... | collective-permute-start | bytes 3145736 | tf_op jit(solution)/shard_map/ppermute | solution.py:396
  65.9 4.2 %collective-permute-start.2 = (f32[512,512]{1,0:T(8,128)}, f32[512,512]{1,0:T(8,128)S(1)}, u32[]{:S(2)}, u32[]{:S(2)}) collective-permute-start(f32[512,512]{1,0:T(8,128)} %get-tuple-element.35), channel_id=1, source_target_pairs={{0,64},{64,0},{128,192},{192,128},{1,65},{65,1},{129,193},{193,129... | collective-permute-start | bytes 3145736 | tf_op jit(solution)/shard_map/ppermute | solution.py:397
  69.9 26.8 %copy-start.3 = (bf16[2,8,64,128]{3,2,1,0:T(8,128)(2,1)}, bf16[2,8,64,128]{3,2,1,0:T(8,128)(2,1)S(1)}, u32[]{:S(2)}) copy-start(bf16[2,8,64,128]{3,2,1,0:T(8,128)(2,1)S(1)} %get-tuple-element.38.near_ref) | copy-start | bytes 786436
  69.9 32.5 %copy-start.1 = (bf16[2,8,64,128]{3,2,1,0:T(8,128)(2,1)}, bf16[2,8,64,128]{3,2,1,0:T(8,128)(2,1)S(1)}, u32[]{:S(2)}) copy-start(bf16[2,8,64,128]{3,2,1,0:T(8,128)(2,1)S(1)} %get-tuple-element.37.near_ref) | copy-start | bytes 786436
  71.0 37.2 %all-to-all-start.1 = ((bf16[64,8,512]{2,1,0:T(8,128)(2,1)}), bf16[64,8,512]{2,1,0:T(8,128)(2,1)S(1)}, u32[]{:S(2)}, u32[]{:S(2)}) async-start(bf16[64,8,512]{2,1,0:T(8,128)(2,1)} %bitcast.11), calls=%async_computation.1 | async-start | bytes 1048576 | tf_op jit(solution)/shard_map/all_to_all | solution.py:405
  76.9 10.6 %collective-permute-start.6 = (bf16[2,8,64,128]{3,2,1,0:T(8,128)(2,1)S(1)}, bf16[2,8,64,128]{3,2,1,0:T(8,128)(2,1)S(1)}, u32[]{:S(2)}, u32[]{:S(2)}) collective-permute-start(bf16[2,8,64,128]{3,2,1,0:T(8,128)(2,1)S(1)} %get-tuple-element.38.near_ref), channel_id=1, source_target_pairs={{0,128},{128,0},{64,192},{192,64},{1,129},{129,1},{65,193},{193,65... | collective-permute-start | bytes 786440 | tf_op jit(solution)/shard_map/ppermute | solution.py:404
  77.4 18.1 %collective-permute-start.3 = (bf16[2,8,64,128]{3,2,1,0:T(8,128)(2,1)S(1)}, bf16[2,8,64,128]{3,2,1,0:T(8,128)(2,1)S(1)}, u32[]{:S(2)}, u32[]{:S(2)}) collective-permute-start(bf16[2,8,64,128]{3,2,1,0:T(8,128)(2,1)S(1)} %get-tuple-element.37.near_ref), channel_id=1, source_target_pairs={{0,128},{128,0},{64,192},{192,64},{1,129},{129,1},{65,193},{193,65... | collective-permute-start | bytes 786440 | tf_op jit(solution)/shard_map/ppermute | solution.py:404
  78.5 18.2 %collective-permute-start.7 = (bf16[2,8,64,128]{3,2,1,0:T(8,128)(2,1)S(1)}, bf16[2,8,64,128]{3,2,1,0:T(8,128)(2,1)S(1)}, u32[]{:S(2)}, u32[]{:S(2)}) collective-permute-start(bf16[2,8,64,128]{3,2,1,0:T(8,128)(2,1)S(1)} %get-tuple-element.38.near_ref), channel_id=1, source_target_pairs={{0,64},{64,0},{128,192},{192,128},{1,65},{65,1},{129,193},{193,129... | collective-permute-start | bytes 786440 | tf_op jit(solution)/shard_map/ppermute | solution.py:407
  87.5 9.2 %copy-start.8 = (bf16[2,8,64,128]{3,2,1,0:T(8,128)(2,1)}, bf16[2,8,64,128]{3,2,1,0:T(8,128)(2,1)S(1)}, u32[]{:S(2)}) copy-start(bf16[2,8,64,128]{3,2,1,0:T(8,128)(2,1)S(1)} %collective-permute-done.6.far_ref) | copy-start | bytes 786436
  87.5 9.2 %collective-permute-start.8 = (bf16[2,8,64,128]{3,2,1,0:T(8,128)(2,1)S(1)}, bf16[2,8,64,128]{3,2,1,0:T(8,128)(2,1)S(1)}, u32[]{:S(2)}, u32[]{:S(2)}) collective-permute-start(bf16[2,8,64,128]{3,2,1,0:T(8,128)(2,1)S(1)} %collective-permute-done.6.far_ref), channel_id=1, source_target_pairs={{0,64},{64,0},{128,192},{192,128},{1,65},{65,1},{129,193},{193,129... | collective-permute-start | bytes 786440 | tf_op jit(solution)/shard_map/ppermute | solution.py:408
  90.4 12.1 %collective-permute-start.4 = (bf16[2,8,64,128]{3,2,1,0:T(8,128)(2,1)S(1)}, bf16[2,8,64,128]{3,2,1,0:T(8,128)(2,1)S(1)}, u32[]{:S(2)}, u32[]{:S(2)}) collective-permute-start(bf16[2,8,64,128]{3,2,1,0:T(8,128)(2,1)S(1)} %get-tuple-element.37.near_ref), channel_id=1, source_target_pairs={{0,64},{64,0},{128,192},{192,128},{1,65},{65,1},{129,193},{193,129... | collective-permute-start | bytes 786440 | tf_op jit(solution)/shard_map/ppermute | solution.py:407
  95.5 6.9 %copy-start.5 = (bf16[2,8,64,128]{3,2,1,0:T(8,128)(2,1)}, bf16[2,8,64,128]{3,2,1,0:T(8,128)(2,1)S(1)}, u32[]{:S(2)}) copy-start(bf16[2,8,64,128]{3,2,1,0:T(8,128)(2,1)S(1)} %collective-permute-done.3.far_ref) | copy-start | bytes 786436
  95.5 6.9 %collective-permute-start.5 = (bf16[2,8,64,128]{3,2,1,0:T(8,128)(2,1)S(1)}, bf16[2,8,64,128]{3,2,1,0:T(8,128)(2,1)S(1)}, u32[]{:S(2)}, u32[]{:S(2)}) collective-permute-start(bf16[2,8,64,128]{3,2,1,0:T(8,128)(2,1)S(1)} %collective-permute-done.3.far_ref), channel_id=1, source_target_pairs={{0,64},{64,0},{128,192},{192,128},{1,65},{65,1},{129,193},{193,129... | collective-permute-start | bytes 786440 | tf_op jit(solution)/shard_map/ppermute | solution.py:408
  96.7 0.8 copy-start.10
  102.5 0.7 copy-start.6
  102.5 0.8 copy-start.7
  108.3 3.7 %copy-start.11 = (f32[8,512]{1,0:T(8,128)}, f32[8,512]{1,0:T(8,128)S(1)}, u32[]{:S(2)}) copy-start(f32[8,512]{1,0:T(8,128)S(1)} %convert_reduce_fusion.own_ref) | copy-start | bytes 49156
  108.3 3.3 %collective-permute-start.11 = (f32[8,512]{1,0:T(8,128)S(1)}, f32[8,512]{1,0:T(8,128)S(1)}, u32[]{:S(2)}, u32[]{:S(2)}) collective-permute-start(f32[8,512]{1,0:T(8,128)S(1)} %convert_reduce_fusion.own_ref), channel_id=1, source_target_pairs={{0,192},{192,0},{64,128},{128,64},{1,193},{193,1},{65,129},{129,65... | collective-permute-start | bytes 49160 | tf_op jit(solution)/shard_map/ppermute | solution.py:415
  108.9 2.7 %collective-permute-start.10 = (f32[8,512]{1,0:T(8,128)S(1)}, f32[8,512]{1,0:T(8,128)S(1)}, u32[]{:S(2)}, u32[]{:S(2)}) collective-permute-start(f32[8,512]{1,0:T(8,128)S(1)} %convert_reduce_fusion.own_ref), channel_id=1, source_target_pairs={{0,64},{64,0},{128,192},{192,128},{1,65},{65,1},{129,193},{193,129... | collective-permute-start | bytes 49160 | tf_op jit(solution)/shard_map/ppermute | solution.py:415
  109.4 2.6 %collective-permute-start.9 = (f32[8,512]{1,0:T(8,128)S(1)}, f32[8,512]{1,0:T(8,128)S(1)}, u32[]{:S(2)}, u32[]{:S(2)}) collective-permute-start(f32[8,512]{1,0:T(8,128)S(1)} %convert_reduce_fusion.own_ref), channel_id=1, source_target_pairs={{0,128},{128,0},{64,192},{192,64},{1,129},{129,1},{65,193},{193,65... | collective-permute-start | bytes 49160 | tf_op jit(solution)/shard_map/ppermute | solution.py:415
  (4 other events, 2.5 us)
where the time goes:
time: 115 us; the launch traced here: 114 us
  blocking collectives  37.6 us (33%)
  Pallas kernels  35.1 us (31%)
  starting transfers between devices  17.8 us (15%)
  waiting for transfers between devices  17.4 us (15%)
  local copies, waits for them, and re-layouts  3.32 us (3%)
  other arithmetic  2.43 us (2%)
    all_to_all x1, blocking collectives, local(): mine = lax.all_to_all(packed, 'dp', split_axis=0, concat_axis=0, tiled=True)  37.6 us
    pallas_call x1, Pallas kernels, terms(): pl.pallas_call(terms_kernel, out_shape=(jax.ShapeDtypeStruct(half, F32),...  15.3 us
    ppermute x2, waiting for transfers between devices, local(): far.append(lax.ppermute(near[h], 'rep', CHIP_SWAP))  13.2 us
    pallas_call x2, Pallas kernels, mid_step(): pl.pallas_call(mid_kernel, grid=(blocks,), out_shape=tuple((jax.ShapeDtyp...  9.82 us
    pallas_call x1, Pallas kernels, mid_round(): pl.pallas_call(mid_copy_kernel, grid=(R // R_BLOCK,), out_shape=jax.Shape...  5.89 us
    all_to_all x1, starting transfers between devices, local(): lax.all_to_all(chip_sum, 'dp', split_axis=0, concat_axis=0, tiled=True)  5.89 us
    ppermute x2, starting transfers between devices, local(): far_rest = lax.ppermute(far[h], 'rep', CORE_SWAP)  3.99 us
    unnamed x30, local copies, waits for them, and re-layouts  3.32 us
  transfers between devices with their start and end apart: 13, of which 6 were waited for; matrix products, arithmetic and copies ran while one was open for 1% of the time, Pallas kernels for 14%

commit v1 on v0

--- a/solution.py
+++ b/solution.py
@@ -17,6 +17,7 @@
 SLOTS = 512
 GROUP = 32
 GROUPS = 16
+BIG = 80
 
 LEARN_RATE = 0.01
 BETA_ONE = 0.9
@@ -114,7 +115,7 @@
 
 def terms_kernel(
     side_ref, mine_ref, theirs_ref, mid_ref,
-    midkeep_ref, midsend_ref, keep_ref, send_ref,
+    keep_big, keep_small, send_big, send_small, keep_ref, send_ref,
     cores, lrows, pick, diag, mix_hi, mix_lo, outer, chosen, asub,
 ):
     side = side_ref[0]
@@ -198,7 +199,7 @@
     for n in range(4):
         half = side if n < 2 else 1 - side
         m = half * 2 + n % 2
-        grad_ref = midkeep_ref if n < 2 else midsend_ref
+        grad_refs = (keep_big, keep_small) if n < 2 else (send_big, send_small)
         span = pl.ds(pl.multiple_of(m * SLOTS, SLOTS), SLOTS)
         left = jnp.concatenate([asub[4 * m + g] for g in range(4)], axis=0)
         part = None
@@ -209,10 +210,9 @@
             term = nt(jnp.concatenate([hi, lo], axis=1), jnp.concatenate([pair, pair], axis=1))
             part = term if part is None else part + term
             grad = tn(left, hi)
-            for h in range(2):
-                tops = slice(h * (R // 2), (h + 1) * (R // 2))
-                grad_ref[h, n % 2, b] = grad[tops, 0:LANES]
-                grad_ref[h, n % 2, b + 1] = grad[tops, LANES:]
+            for grad_ref, tops in zip(grad_refs, (slice(0, BIG), slice(BIG, R))):
+                grad_ref[n % 2, b] = grad[tops, 0:LANES]
+                grad_ref[n % 2, b + 1] = grad[tops, LANES:]
         for q in range(4):
             for a in range(D1):
                 here = pl.ds(pl.multiple_of((4 * m + q) * GROUP, GROUP), GROUP)
@@ -227,17 +227,19 @@
 def terms(side, mine, theirs, mid):
     vmem = pl.BlockSpec(memory_space=pltpu.VMEM)
     width = D1 * R
-    half = (2, 2, D2, R // 2, LANES)
+    big, small = (2, D2, BIG, LANES), (2, D2, R - BIG, LANES)
     return pl.pallas_call(
         terms_kernel,
         out_shape=(
-            jax.ShapeDtypeStruct(half, F32),
-            jax.ShapeDtypeStruct(half, F32),
+            jax.ShapeDtypeStruct(big, F32),
+            jax.ShapeDtypeStruct(small, F32),
+            jax.ShapeDtypeStruct(big, F32),
+            jax.ShapeDtypeStruct(small, F32),
             jax.ShapeDtypeStruct((SLOTS, width), F32),
             jax.ShapeDtypeStruct((SLOTS, width), F32),
         ),
         in_specs=[pl.BlockSpec(memory_space=pltpu.SMEM)] + [vmem] * 3,
-        out_specs=(vmem,) * 4,
+        out_specs=(vmem,) * 6,
         scratch_shapes=[
             pltpu.VMEM((2, SLOTS, width), BF),
             pltpu.VMEM((GROUPS, D3 * GROUP, LANES), BF),
@@ -295,8 +297,8 @@
 
 def mid_step(side, states, parts, h, begun):
     rows = R_BLOCK * D2 * 4
-    blocks = R // R_BLOCK // 2
-    state = pl.BlockSpec((rows, LANES), lambda i: (i + h * blocks, 0))
+    blocks = (R - BIG if h else BIG) // R_BLOCK
+    state = pl.BlockSpec((rows, LANES), lambda i: (i + h * (BIG // R_BLOCK), 0))
     part = pl.BlockSpec((2, D2, R_BLOCK, LANES), lambda i: (0, 0, i, 0))
     untouched = [pl.BlockSpec(memory_space=pl.ANY)] * len(begun)
     return pl.pallas_call(
@@ -391,11 +393,11 @@
     mine = lax.all_to_all(packed, "dp", split_axis=0, concat_axis=0, tiled=True)
     mid_copy = mid_round(mid_rows)
     theirs = lax.ppermute(mine, "rep", CORE_SWAP)
-    mid_keep, mid_send, keep, send = terms(side, mine, theirs, mid_copy)
-
-    mid_other = lax.ppermute(mid_send, "rep", CORE_SWAP)
+    *mids, keep, send = terms(side, mine, theirs, mid_copy)
+
+    mid_other = [lax.ppermute(x, "rep", CORE_SWAP) for x in mids[2:]]
     other = lax.ppermute(send, "rep", CORE_SWAP)
-    near = [(mid_keep[h] + mid_other[h]).astype(BF) for h in range(2)]
+    near = [(mids[h] + mid_other[h]).astype(BF) for h in range(2)]
     *near, chip_sum = lax.optimization_barrier((*near, (keep + other).astype(BF)))
     states = (mid_rows, row_tiles(mid_moment), row_tiles(mid_second))
     mid_next = ()

time: 115 us -> 118 us (1.026)
    ppermute x1 -> x2, waiting for transfers between devices: 2.36 us -> 3.68 us  [local(): mid_other = [lax.ppermute(x, 'rep', CORE_SWAP) for x in mids[2:]]]
  transfers between devices with their start and end apart: 13 -> 14, of which waited for: 6 -> 5; matrix products, arithmetic and copies ran while one was open for 1% -> 2% of each run, Pallas kernels for 14% -> 14%
where the time goes in v1:
time: 118 us
  blocking collectives  37.6 us (32%)
  Pallas kernels  35.9 us (30%)
  starting transfers between devices  18.4 us (16%)
  waiting for transfers between devices  18.2 us (15%)
  other arithmetic  3.33 us (3%)
  local copies, waits for them, and re-layouts  3.3 us (3%)
    all_to_all x1, blocking collectives, local(): mine = lax.all_to_all(packed, 'dp', split_axis=0, concat_axis=0, tiled=True)  37.6 us
    pallas_call x1, Pallas kernels, terms(): pl.pallas_call(terms_kernel, out_shape=(jax.ShapeDtypeStruct(big, F32), j...  15.3 us
    ppermute x2, waiting for transfers between devices, local(): far.append(lax.ppermute(near[h], 'rep', CHIP_SWAP))  12.8 us
    pallas_call x2, Pallas kernels, mid_step(): pl.pallas_call(mid_kernel, grid=(blocks,), out_shape=tuple((jax.ShapeDtyp...  10.7 us
    pallas_call x1, Pallas kernels, mid_round(): pl.pallas_call(mid_copy_kernel, grid=(R // R_BLOCK,), out_shape=jax.Shape...  5.89 us
    all_to_all x1, starting transfers between devices, local(): lax.all_to_all(chip_sum, 'dp', split_axis=0, concat_axis=0, tiled=True)  5.89 us
    ppermute x2, starting transfers between devices, local(): far_rest = lax.ppermute(far[h], 'rep', CORE_SWAP)  4.27 us
    ppermute x2, waiting for transfers between devices, local(): mid_other = [lax.ppermute(x, 'rep', CORE_SWAP) for x in mids[2:]]  3.68 us
  transfers between devices with their start and end apart: 14, of which 5 were waited for; matrix products, arithmetic and copies ran while one was open for 2% of the time, Pallas kernels for 14%

profile of v1, /device:TPU:1, one launch (start us, length us, event | category | flops | bytes accessed | tf_op | source)
XLA Modules:
  0.0 117.6 jit_solution(18137097237610285754)
XLA Ops:
  0.7 2.4 %pack.1 = bf16[512,768]{1,0:T(8,128)(2,1)} custom-call(s32[1]{0:T(128)} %bitcast.side_ref, s32[1,256]{1,0:T(1,128)} %bitcast.55, s32[1,256]{1,0:T(1,128)} %bitcast.56, s32[1,256]{1,0:T(1,128)} %bitcast.57, s32[1,16]{1,0:T(1,128)} %bag_ref.1, bf16[16,128]{1,0:T(8,128)(2,1)} %cot_ref.1, f32[8,512]{1,0:T(8,128)} %refs_0_.1, f32[8,512]{1,0:T(8,128)} %refs_3_.1), custom_call_target="tpu_custom_call" | custom-call | tf_op jit(solution)/shard_map/pack/pallas_call | solution.py:106
  3.0 37.6 %all_to_all.23 = bf16[64,8,768]{2,1,0:T(8,128)(2,1)S(1)} all-to-all(bf16[64,8,768]{2,1,0:T(8,128)(2,1)} %bitcast.48), channel_id=1, replica_groups=mesh['rep'=4,'dp'=64] {'dp'}, dimensions={0} | all-to-all | bytes 1572864 | tf_op jit(solution)/shard_map/all_to_all | solution.py:393
  40.7 2.9 %collective-permute-start = (bf16[512,768]{1,0:T(8,128)(2,1)S(1)}, bf16[512,768]{1,0:T(8,128)(2,1)S(1)}, u32[]{:S(2)}, u32[]{:S(2)}) collective-permute-start(bf16[512,768]{1,0:T(8,128)(2,1)S(1)} %bitcast.49), channel_id=1, source_target_pairs={{0,64},{64,0},{128,192},{192,128},{1,65},{65,1},{129,193},{193,129... | collective-permute-start | bytes 2359304 | tf_op jit(solution)/shard_map/ppermute | solution.py:395
  43.5 5.9 %mid_round.1.mid_ref = bf16[4,8,128,128]{3,2,1,0:T(8,128)(2,1)} custom-call(f32[4096,128]{1,0:T(8,128)} %bitcast.41), custom_call_target="tpu_custom_call" | custom-call | tf_op jit(solution)/shard_map/mid_round/pallas_call | solution.py:269
  49.4 0.9 copy-done.3
  50.4 15.3 %terms.1 = (f32[2,8,80,128]{3,2,1,0:T(8,128)}, f32[2,8,48,128]{3,2,1,0:T(8,128)}, f32[2,8,80,128]{3,2,1,0:T(8,128)}, f32[2,8,48,128]{3,2,1,0:T(8,128)}, f32[512,512]{1,0:T(8,128)}, /*index=5*/f32[512,512]{1,0:T(8,128)}) custom-call(s32[1]{0:T(128)} %bitcast.side_ref, bf16[512,768]{1,0:T(8,128)(2,1)} %bitcast.50, bf16[512,768]{1,0:T(8,128)(2,1)} %copy-done.3, ...), custom_call_target="tpu_custom_call" | custom-call | tf_op jit(solution)/shard_map/terms/pallas_call | solution.py:231
  66.4 3.7 %collective-permute-done.2 = f32[2,8,48,128]{3,2,1,0:T(8,128)S(1)} collective-permute-done((f32[2,8,48,128]{3,2,1,0:T(8,128)}, f32[2,8,48,128]{3,2,1,0:T(8,128)S(1)}, u32[]{:S(2)}, u32[]{:S(2)}) %collective-permute-start.2) | collective-permute-done | bytes 393248 | tf_op jit(solution)/shard_map/ppermute | solution.py:398
  70.1 1.0 add_convert_fusion.2.near_ref
  71.1 1.2 %add_convert_fusion.1.near_ref = bf16[2,8,80,128]{3,2,1,0:T(8,128)(2,1)S(1)} fusion(f32[2,8,80,128]{3,2,1,0:T(8,128)} %get-tuple-element.34, f32[2,8,80,128]{3,2,1,0:T(8,128)S(1)} %collective-permute-done.1), kind=kLoop, calls=%fused_computation.2 | loop fusion | flops 327680 | bytes 1638400 | tf_op jit(solution)/shard_map/convert_element_type | solution.py:400
  72.4 1.0 add_convert_fusion
  73.4 5.9 %all-to-all-start.1 = ((bf16[64,8,512]{2,1,0:T(8,128)(2,1)}), bf16[64,8,512]{2,1,0:T(8,128)(2,1)S(1)}, u32[]{:S(2)}, u32[]{:S(2)}) async-start(bf16[64,8,512]{2,1,0:T(8,128)(2,1)} %bitcast.9), calls=%async_computation.1 | async-start | bytes 1048576 | tf_op jit(solution)/shard_map/all_to_all | solution.py:407
  79.7 1.1 collective-permute-start.4
  80.8 1.0 collective-permute-start.8
  81.9 10.3 %collective-permute-done.7.far_ref = bf16[2,8,80,128]{3,2,1,0:T(8,128)(2,1)S(1)} collective-permute-done((bf16[2,8,80,128]{3,2,1,0:T(8,128)(2,1)S(1)}, bf16[2,8,80,128]{3,2,1,0:T(8,128)(2,1)S(1)}, u32[]{:S(2)}, u32[]{:S(2)}) %collective-permute-start.7) | collective-permute-done | bytes 327712 | tf_op jit(solution)/shard_map/ppermute | solution.py:406
  92.2 3.1 %collective-permute-start.9 = (bf16[2,8,80,128]{3,2,1,0:T(8,128)(2,1)S(1)}, bf16[2,8,80,128]{3,2,1,0:T(8,128)(2,1)S(1)}, u32[]{:S(2)}, u32[]{:S(2)}) collective-permute-start(bf16[2,8,80,128]{3,2,1,0:T(8,128)(2,1)S(1)} %collective-permute-done.7.far_ref), channel_id=1, source_target_pairs={{0,64},{64,0},{128,192},{192,128},{1,65},{65,1},{129,193},{193,129... | collective-permute-start | bytes 983048 | tf_op jit(solution)/shard_map/ppermute | solution.py:410
  95.4 2.5 %collective-permute-done.4.far_ref = bf16[2,8,48,128]{3,2,1,0:T(8,128)(2,1)S(1)} collective-permute-done((bf16[2,8,48,128]{3,2,1,0:T(8,128)(2,1)S(1)}, bf16[2,8,48,128]{3,2,1,0:T(8,128)(2,1)S(1)}, u32[]{:S(2)}, u32[]{:S(2)}) %collective-permute-start.4) | collective-permute-done | bytes 196640 | tf_op jit(solution)/shard_map/ppermute | solution.py:406
  97.9 1.2 collective-permute-start.6
  99.1 0.7 copy-done.6
  99.9 6.3 %mid_step.2 = (f32[4096,128]{1,0:T(8,128)}, f32[4096,128]{1,0:T(8,128)}, f32[4096,128]{1,0:T(8,128)}) custom-call(s32[1]{0:T(128)} %bitcast.side_ref, f32[4096,128]{1,0:T(8,128)} %bitcast.42, f32[4096,128]{1,0:T(8,128)} %bitcast.44, f32[4096,128]{1,0:T(8,128)} %bitcast.46, bf16[2,8,80,128]{3,2,1,0:T(8,128)(2,1)} %copy-done.1, ...), custom_call_target="tpu_custom_call" | custom-call | tf_op jit(solution)/shard_map/mid_step/pallas_call | solution.py:304
  106.3 0.6 copy-done.9
  107.0 4.3 %mid_step.3 = (f32[4096,128]{1,0:T(8,128)}, f32[4096,128]{1,0:T(8,128)}, f32[4096,128]{1,0:T(8,128)}) custom-call(s32[1]{0:T(128)} %bitcast.side_ref, f32[4096,128]{1,0:T(8,128)} %bitcast.43, f32[4096,128]{1,0:T(8,128)} %bitcast.45, f32[4096,128]{1,0:T(8,128)} %bitcast.47, ...), custom_call_target="tpu_custom_call", output_to_operand_aliasing={{0}: (8, {}), {1}: (9, {}), {2}: (10, {})} | custom-call | tf_op jit(solution)/shard_map/mid_step/pallas_call | solution.py:304
  112.5 0.9 collective-permute-start.10
  113.4 1.3 %collective-permute-done.12.both_ref = f32[8,512]{1,0:T(8,128)S(1)} collective-permute-done((f32[8,512]{1,0:T(8,128)S(1)}, f32[8,512]{1,0:T(8,128)S(1)}, u32[]{:S(2)}, u32[]{:S(2)}) %collective-permute-start.12) | collective-permute-done | bytes 16416 | tf_op jit(solution)/shard_map/ppermute | solution.py:417
  115.9 1.7 %outer.1 = (f32[8,512]{1,0:T(8,128)}, f32[8,512]{1,0:T(8,128)}, f32[8,512]{1,0:T(8,128)}, f32[8,512]{1,0:T(8,128)}, f32[8,512]{1,0:T(8,128)}, /*index=5*/f32[8,512]{1,0:T(8,128)}) custom-call(s32[1]{0:T(128)} %bitcast.side_ref, f32[8,512]{1,0:T(8,128)} %copy-done.11, f32[8,512]{1,0:T(8,128)} %copy-done.14, f32[8,512]{1,0:T(8,128)} %copy-done.13, ...), custom_call_target="tpu_custom_call" | custom-call | tf_op jit(solution)/shard_map/outer/pallas_call | solution.py:342
  (45 shorter events, 3.9 us)
Async XLA Ops:
  40.7 8.8 %copy-start = (bf16[64,8,768]{2,1,0:T(8,128)(2,1)}, bf16[64,8,768]{2,1,0:T(8,128)(2,1)S(1)}, u32[]{:S(2)}) copy-start(bf16[64,8,768]{2,1,0:T(8,128)(2,1)S(1)} %all_to_all.23) | copy-start | bytes 2359300
  40.7 8.8 %collective-permute-start = (bf16[512,768]{1,0:T(8,128)(2,1)S(1)}, bf16[512,768]{1,0:T(8,128)(2,1)S(1)}, u32[]{:S(2)}, u32[]{:S(2)}) collective-permute-start(bf16[512,768]{1,0:T(8,128)(2,1)S(1)} %bitcast.49), channel_id=1, source_target_pairs={{0,64},{64,0},{128,192},{192,128},{1,65},{65,1},{129,193},{193,129... | collective-permute-start | bytes 2359304 | tf_op jit(solution)/shard_map/ppermute | solution.py:395
  49.4 0.9 copy-start.3
  65.7 6.7 %copy-start.2 = (f32[512,512]{1,0:T(8,128)S(1)}, f32[512,512]{1,0:T(8,128)}, u32[]{:S(2)}) copy-start(f32[512,512]{1,0:T(8,128)} %get-tuple-element.38) | copy-start | bytes 3145732
  65.7 6.7 %collective-permute-start.3 = (f32[512,512]{1,0:T(8,128)}, f32[512,512]{1,0:T(8,128)S(1)}, u32[]{:S(2)}, u32[]{:S(2)}) collective-permute-start(f32[512,512]{1,0:T(8,128)} %get-tuple-element.39), channel_id=1, source_target_pairs={{0,64},{64,0},{128,192},{192,128},{1,65},{65,1},{129,193},{193,129... | collective-permute-start | bytes 3145736 | tf_op jit(solution)/shard_map/ppermute | solution.py:399
  65.9 5.2 %collective-permute-start.1 = (f32[2,8,80,128]{3,2,1,0:T(8,128)}, f32[2,8,80,128]{3,2,1,0:T(8,128)S(1)}, u32[]{:S(2)}, u32[]{:S(2)}) collective-permute-start(f32[2,8,80,128]{3,2,1,0:T(8,128)} %get-tuple-element.35), channel_id=1, source_target_pairs={{0,64},{64,0},{128,192},{192,128},{1,65},{65,1},{129,193},{193,129... | collective-permute-start | bytes 1966088 | tf_op jit(solution)/shard_map/ppermute | solution.py:398
  66.2 3.9 %collective-permute-start.2 = (f32[2,8,48,128]{3,2,1,0:T(8,128)}, f32[2,8,48,128]{3,2,1,0:T(8,128)S(1)}, u32[]{:S(2)}, u32[]{:S(2)}) collective-permute-start(f32[2,8,48,128]{3,2,1,0:T(8,128)} %get-tuple-element.37), channel_id=1, source_target_pairs={{0,64},{64,0},{128,192},{192,128},{1,65},{65,1},{129,193},{193,129... | collective-permute-start | bytes 1179656 | tf_op jit(solution)/shard_map/ppermute | solution.py:398
  71.1 24.2 %copy-start.4 = (bf16[2,8,48,128]{3,2,1,0:T(8,128)(2,1)}, bf16[2,8,48,128]{3,2,1,0:T(8,128)(2,1)S(1)}, u32[]{:S(2)}) copy-start(bf16[2,8,48,128]{3,2,1,0:T(8,128)(2,1)S(1)} %add_convert_fusion.2.near_ref) | copy-start | bytes 589828
  72.4 26.7 %copy-start.1 = (bf16[2,8,80,128]{3,2,1,0:T(8,128)(2,1)}, bf16[2,8,80,128]{3,2,1,0:T(8,128)(2,1)S(1)}, u32[]{:S(2)}) copy-start(bf16[2,8,80,128]{3,2,1,0:T(8,128)(2,1)S(1)} %add_convert_fusion.1.near_ref) | copy-start | bytes 983044
  73.4 37.9 %all-to-all-start.1 = ((bf16[64,8,512]{2,1,0:T(8,128)(2,1)}), bf16[64,8,512]{2,1,0:T(8,128)(2,1)S(1)}, u32[]{:S(2)}, u32[]{:S(2)}) async-start(bf16[64,8,512]{2,1,0:T(8,128)(2,1)} %bitcast.9), calls=%async_computation.1 | async-start | bytes 1048576 | tf_op jit(solution)/shard_map/all_to_all | solution.py:407
  79.3 12.9 %collective-permute-start.7 = (bf16[2,8,80,128]{3,2,1,0:T(8,128)(2,1)S(1)}, bf16[2,8,80,128]{3,2,1,0:T(8,128)(2,1)S(1)}, u32[]{:S(2)}, u32[]{:S(2)}) collective-permute-start(bf16[2,8,80,128]{3,2,1,0:T(8,128)(2,1)S(1)} %add_convert_fusion.1.near_ref), channel_id=1, source_target_pairs={{0,128},{128,0},{64,192},{192,64},{1,129},{129,1},{65,193},{193,65... | collective-permute-start | bytes 983048 | tf_op jit(solution)/shard_map/ppermute | solution.py:406
  79.7 18.1 %collective-permute-start.4 = (bf16[2,8,48,128]{3,2,1,0:T(8,128)(2,1)S(1)}, bf16[2,8,48,128]{3,2,1,0:T(8,128)(2,1)S(1)}, u32[]{:S(2)}, u32[]{:S(2)}) collective-permute-start(bf16[2,8,48,128]{3,2,1,0:T(8,128)(2,1)S(1)} %add_convert_fusion.2.near_ref), channel_id=1, source_target_pairs={{0,128},{128,0},{64,192},{192,64},{1,129},{129,1},{65,193},{193,65... | collective-permute-start | bytes 589832 | tf_op jit(solution)/shard_map/ppermute | solution.py:406
  80.8 18.2 %collective-permute-start.8 = (bf16[2,8,80,128]{3,2,1,0:T(8,128)(2,1)S(1)}, bf16[2,8,80,128]{3,2,1,0:T(8,128)(2,1)S(1)}, u32[]{:S(2)}, u32[]{:S(2)}) collective-permute-start(bf16[2,8,80,128]{3,2,1,0:T(8,128)(2,1)S(1)} %add_convert_fusion.1.near_ref), channel_id=1, source_target_pairs={{0,64},{64,0},{128,192},{192,128},{1,65},{65,1},{129,193},{193,129... | collective-permute-start | bytes 983048 | tf_op jit(solution)/shard_map/ppermute | solution.py:409
  92.2 6.9 %copy-start.5 = (bf16[2,8,80,128]{3,2,1,0:T(8,128)(2,1)}, bf16[2,8,80,128]{3,2,1,0:T(8,128)(2,1)S(1)}, u32[]{:S(2)}) copy-start(bf16[2,8,80,128]{3,2,1,0:T(8,128)(2,1)S(1)} %collective-permute-done.7.far_ref) | copy-start | bytes 983044
  92.2 6.9 %collective-permute-start.9 = (bf16[2,8,80,128]{3,2,1,0:T(8,128)(2,1)S(1)}, bf16[2,8,80,128]{3,2,1,0:T(8,128)(2,1)S(1)}, u32[]{:S(2)}, u32[]{:S(2)}) collective-permute-start(bf16[2,8,80,128]{3,2,1,0:T(8,128)(2,1)S(1)} %collective-permute-done.7.far_ref), channel_id=1, source_target_pairs={{0,64},{64,0},{128,192},{192,128},{1,65},{65,1},{129,193},{193,129... | collective-permute-start | bytes 983048 | tf_op jit(solution)/shard_map/ppermute | solution.py:410
  95.3 10.9 %collective-permute-start.5 = (bf16[2,8,48,128]{3,2,1,0:T(8,128)(2,1)S(1)}, bf16[2,8,48,128]{3,2,1,0:T(8,128)(2,1)S(1)}, u32[]{:S(2)}, u32[]{:S(2)}) collective-permute-start(bf16[2,8,48,128]{3,2,1,0:T(8,128)(2,1)S(1)} %add_convert_fusion.2.near_ref), channel_id=1, source_target_pairs={{0,64},{64,0},{128,192},{192,128},{1,65},{65,1},{129,193},{193,129... | collective-permute-start | bytes 589832 | tf_op jit(solution)/shard_map/ppermute | solution.py:409
  97.9 8.4 %copy-start.8 = (bf16[2,8,48,128]{3,2,1,0:T(8,128)(2,1)}, bf16[2,8,48,128]{3,2,1,0:T(8,128)(2,1)S(1)}, u32[]{:S(2)}) copy-start(bf16[2,8,48,128]{3,2,1,0:T(8,128)(2,1)S(1)} %collective-permute-done.4.far_ref) | copy-start | bytes 589828
  97.9 8.4 %collective-permute-start.6 = (bf16[2,8,48,128]{3,2,1,0:T(8,128)(2,1)S(1)}, bf16[2,8,48,128]{3,2,1,0:T(8,128)(2,1)S(1)}, u32[]{:S(2)}, u32[]{:S(2)}) collective-permute-start(bf16[2,8,48,128]{3,2,1,0:T(8,128)(2,1)S(1)} %collective-permute-done.4.far_ref), channel_id=1, source_target_pairs={{0,64},{64,0},{128,192},{192,128},{1,65},{65,1},{129,193},{193,129... | collective-permute-start | bytes 589832 | tf_op jit(solution)/shard_map/ppermute | solution.py:410
  99.1 0.7 copy-start.6
  99.1 0.8 copy-start.7
  111.4 3.7 %copy-start.11 = (f32[8,512]{1,0:T(8,128)}, f32[8,512]{1,0:T(8,128)S(1)}, u32[]{:S(2)}) copy-start(f32[8,512]{1,0:T(8,128)S(1)} %convert_reduce_fusion.own_ref) | copy-start | bytes 49156
  111.4 3.3 %collective-permute-start.12 = (f32[8,512]{1,0:T(8,128)S(1)}, f32[8,512]{1,0:T(8,128)S(1)}, u32[]{:S(2)}, u32[]{:S(2)}) collective-permute-start(f32[8,512]{1,0:T(8,128)S(1)} %convert_reduce_fusion.own_ref), channel_id=1, source_target_pairs={{0,192},{192,0},{64,128},{128,64},{1,193},{193,1},{65,129},{129,65... | collective-permute-start | bytes 49160 | tf_op jit(solution)/shard_map/ppermute | solution.py:417
  112.0 2.7 %collective-permute-start.11 = (f32[8,512]{1,0:T(8,128)S(1)}, f32[8,512]{1,0:T(8,128)S(1)}, u32[]{:S(2)}, u32[]{:S(2)}) collective-permute-start(f32[8,512]{1,0:T(8,128)S(1)} %convert_reduce_fusion.own_ref), channel_id=1, source_target_pairs={{0,64},{64,0},{128,192},{192,128},{1,65},{65,1},{129,193},{193,129... | collective-permute-start | bytes 49160 | tf_op jit(solution)/shard_map/ppermute | solution.py:417
  112.5 2.6 %collective-permute-start.10 = (f32[8,512]{1,0:T(8,128)S(1)}, f32[8,512]{1,0:T(8,128)S(1)}, u32[]{:S(2)}, u32[]{:S(2)}) collective-permute-start(f32[8,512]{1,0:T(8,128)S(1)} %convert_reduce_fusion.own_ref), channel_id=1, source_target_pairs={{0,128},{128,0},{64,192},{192,64},{1,129},{129,1},{65,193},{193,65... | collective-permute-start | bytes 49160 | tf_op jit(solution)/shard_map/ppermute | solution.py:417
  (5 other events, 3.2 us)
